TPU v7x, 32 devices: a whole 2x2x4 slice. The times are simulated.
32 devices in a mesh: batch: 4 (over z), seq: 2 (over core), ch: 4 (over y, x).
Axes of the slice: x: 2, y: 2, z: 4, core: 2. Of those that a mesh axis runs over, the one named last changes fastest.
Arguments:
- inputs: bfloat16 [16, 1280, 2048], P('batch', 'ch', 'seq'), may hold values from -6 to 6
- segment_ids: int32 [16, 2048], P('batch', 'seq'), may hold values from 0 to 7, never falling along the last dimension, each value on 1 to 512 neighbouring positions
- norm0_gain: float32 [1280], P('ch'), may hold values from 0.1 to 1.9
- norm0_shift: float32 [1280], P('ch'), may hold values from -3 to 3
- w_inner: bfloat16 [1280, 640], P('ch'), may hold values from -0.15625 to 0.15625
- b_inner: float32 [640], P('ch'), may hold values from -3 to 3
- norm1_gain: float32 [640], P('ch'), may hold values from 0.1 to 1.9
- norm1_shift: float32 [640], P('ch'), may hold values from -3 to 3
- w_conv: bfloat16 [5, 640, 640], P(None, 'ch'), may hold values from -0.109375 to 0.109375
- b_conv: float32 [640], P('ch'), may hold values from -3 to 3
- norm2_gain: float32 [640], P('ch'), may hold values from 0.1 to 1.9
- norm2_shift: float32 [640], P('ch'), may hold values from -3 to 3
- w_outer: bfloat16 [640, 1280], P('ch'), may hold values from -0.25 to 0.25
- b_outer: float32 [1280], P('ch'), may hold values from -3 to 3
- cotangent: bfloat16 [16, 1280, 2048], P('batch', 'ch', 'seq'), may hold values from -6 to 6
Outputs:
- output: bfloat16 [16, 1280, 2048], P('batch', 'ch', 'seq')
- input_grad: bfloat16 [16, 1280, 2048], P('batch', 'ch', 'seq')
- grad_norm0_gain: float32 [1280], P('ch')
- grad_norm0_shift: float32 [1280], P('ch')
- grad_w_inner: float32 [1280, 640], P('ch')
- grad_b_inner: float32 [640], P('ch')
- grad_norm1_gain: float32 [640], P('ch')
- grad_norm1_shift: float32 [640], P('ch')
- grad_w_conv: float32 [5, 640, 640], P(None, 'ch')
- grad_b_conv: float32 [640], P('ch')
- grad_norm2_gain: float32 [640], P('ch')
- grad_norm2_shift: float32 [640], P('ch')
- grad_w_outer: float32 [640, 1280], P('ch')
- grad_b_outer: float32 [1280], P('ch')
Inputs may be any that keep to these rules, and one draw needn't show every extreme that they name: `segment_ids`: along a row the ids never fall; each protein is one run of 1 to 512 residues, one run of each row has exactly 512, and every row holds all 8 ids.
All inputs are finite; a program needn't handle non-finite values.
Results may differ from a plain program's by a relative error of at most 0.0065.
Values may be sent and summed in bfloat16 or wider, within the bound.
A program may use at most 192 MiB of HBM per device.

v0:
```python
import jax
import jax.numpy as jnp
from jax import lax
from jax.sharding import PartitionSpec as P

KERNEL_TAPS = 5
DILATION_SPACING = 32
EPSILON = 1e-05


def gelu_exact(values):
    return jax.nn.gelu(values, approximate=False)


def gelu_back(point, grad):
    return jax.vjp(gelu_exact, point)[1](grad)[0]


def normalize(values, gain, shift):
    center = jnp.mean(values, axis=1, keepdims=True)
    offset = values - center
    spread = jnp.mean(offset * offset, axis=1, keepdims=True)
    scale = lax.rsqrt(spread + EPSILON)
    unit = offset * scale
    return (unit * gain[:, None] + shift[:, None], unit, scale)


def normalize_back(grad, unit, scale, gain):
    scaled = grad * gain[:, None]
    first = jnp.mean(scaled, axis=1, keepdims=True)
    second = jnp.mean(scaled * unit, axis=1, keepdims=True)
    return scale * (scaled - first - unit * second)


def neighbour_pairs(seqs, nch, q_count):
    pairs = []
    for s in range(seqs):
        for c in range(nch):
            q = c % q_count
            if q < q_count - 1:
                pairs.append((s * nch + c, s * nch + c + 1))
            elif s < seqs - 1:
                pairs.append((s * nch + c, (s + 1) * nch + c - (q_count - 1)))
    return pairs


def extended(x, width, pairs):
    down = [(j, i) for i, j in pairs]
    length = x.shape[-1]
    before = lax.ppermute(x[..., length - width :], ("seq", "ch"), pairs)
    after = lax.ppermute(x[..., :width], ("seq", "ch"), down)
    return jnp.concatenate([before, x, after], axis=-1)


def shifted_taps(wide, wide_ids, own_ids, offsets, border):
    length = own_ids.shape[-1]
    pieces = []
    for offset in offsets:
        lower = border + offset
        shifted = wide[:, :, lower : lower + length]
        matching = wide_ids[:, lower : lower + length] == own_ids
        pieces.append(jnp.where(matching[:, None, :], shifted, jnp.zeros_like(shifted)))
    return jnp.concatenate(pieces, axis=1)


def to_positions(x, nch, q_count):
    rows, width, length = x.shape
    if q_count > 1:
        x = x.reshape(rows, width, q_count, length // q_count).transpose(0, 2, 1, 3)
        x = x.reshape(rows * q_count, width, length // q_count)
    return lax.all_to_all(x, "ch", 0, 1, tiled=True)


def to_channels(x, nch, q_count, rows):
    x = lax.all_to_all(x, "ch", 1, 0, tiled=True)
    if q_count > 1:
        _, width, part = x.shape
        x = (
            x.reshape(rows, q_count, width, part)
            .transpose(0, 2, 1, 3)
            .reshape(rows, width, q_count * part)
        )
    return x


def local(
    inputs,
    segment_ids,
    norm0_gain,
    norm0_shift,
    w_inner,
    b_inner,
    norm1_gain,
    norm1_shift,
    w_conv,
    b_conv,
    norm2_gain,
    norm2_shift,
    w_outer,
    b_outer,
    cotangent,
):
    nch = lax.axis_size("ch")
    seqs = lax.axis_size("seq")
    batches = lax.axis_size("batch")
    rows, dloc, length = inputs.shape
    hloc = w_conv.shape[1]
    hid = hloc * nch
    dim = dloc * nch
    if rows % nch == 0:
        q_count = 1
    else:
        q_count = nch // rows
    part = length // q_count
    border = 2 * DILATION_SPACING
    offsets = [(k - KERNEL_TAPS // 2) * DILATION_SPACING for k in range(KERNEL_TAPS)]
    back_offsets = [-o for o in offsets]
    pairs = neighbour_pairs(seqs, nch, q_count)
    me = lax.axis_index("ch")
    smalls = [
        norm0_gain,
        norm0_shift,
        b_inner,
        norm1_gain,
        norm1_shift,
        b_conv,
        norm2_gain,
        norm2_shift,
        b_outer,
    ]
    small_all = lax.all_gather(jnp.concatenate(smalls), "ch", axis=0, tiled=False)
    cut = 0
    full = []
    for s in smalls:
        n = s.shape[0]
        full.append(small_all[:, cut : cut + n].reshape(n * nch))
        cut += n
    g0, s0, b_in, g1, s1, b_cv, g2, s2, b_out = full
    packed = jnp.concatenate([w_inner.reshape(-1), w_conv.reshape(-1), w_outer.reshape(-1)])
    packed_all = lax.all_gather(packed.reshape(1, -1, 128), "ch", axis=0, tiled=True).reshape(
        nch, -1
    )
    n_in, n_cv = (w_inner.size, w_conv.size)
    w_in = packed_all[:, :n_in].reshape(dim, hid)
    w_cv = (
        packed_all[:, n_in : n_in + n_cv]
        .reshape(nch, KERNEL_TAPS, hloc, hid)
        .transpose(1, 0, 2, 3)
        .reshape(KERNEL_TAPS, hid, hid)
    )
    w_out = packed_all[:, n_in + n_cv :].reshape(hid, dim)
    x = to_positions(inputs, nch, q_count)
    cot = to_positions(cotangent, nch, q_count)
    prow = x.shape[0]
    if q_count == 1:
        ids = lax.dynamic_slice_in_dim(segment_ids, me * prow, prow, axis=0)
    else:
        ids = lax.dynamic_slice_in_dim(segment_ids, me // q_count, 1, axis=0)
        ids = lax.dynamic_slice_in_dim(ids, me % q_count * part, part, axis=1)
    own_ids = ids + 1
    wide_ids = extended(own_ids, border, pairs)
    residual = x.astype(jnp.float32)
    normed0, unit0, scale0 = normalize(residual, g0, s0)
    hidden0 = gelu_exact(normed0).astype(jnp.bfloat16)
    inner = (
        jnp.einsum("dh,rdl->rhl", w_in, hidden0, preferred_element_type=jnp.float32) + b_in[:, None]
    )
    normed1, unit1, scale1 = normalize(inner, g1, s1)
    hidden1 = gelu_exact(normed1).astype(jnp.bfloat16)
    wide_hidden = extended(hidden1, border, pairs)
    taps = shifted_taps(wide_hidden, wide_ids, own_ids, offsets, border)
    kernel_flat = w_cv.reshape(KERNEL_TAPS * hid, hid)
    mixed = (
        jnp.einsum("co,rcl->rol", kernel_flat, taps, preferred_element_type=jnp.float32)
        + b_cv[:, None]
    )
    normed2, unit2, scale2 = normalize(mixed, g2, s2)
    hidden2 = gelu_exact(normed2).astype(jnp.bfloat16)
    branch = jnp.einsum("hd,rhl->rdl", w_out, hidden2, preferred_element_type=jnp.float32)
    output = (residual + branch + b_out[:, None]).astype(jnp.bfloat16)
    grad_b_outer = jnp.sum(cot.astype(jnp.float32), axis=(0, 2))
    grad_w_outer = jnp.einsum("rhl,rdl->hd", hidden2, cot, preferred_element_type=jnp.float32)
    grad_hidden2 = jnp.einsum("hd,rdl->rhl", w_out, cot, preferred_element_type=jnp.float32)
    grad_normed2 = gelu_back(normed2, grad_hidden2)
    grad_norm2_gain = jnp.sum(grad_normed2 * unit2, axis=(0, 2))
    grad_norm2_shift = jnp.sum(grad_normed2, axis=(0, 2))
    grad_mixed = normalize_back(grad_normed2, unit2, scale2, g2).astype(jnp.bfloat16)
    grad_b_conv = jnp.sum(grad_mixed.astype(jnp.float32), axis=(0, 2))
    grad_w_conv = jnp.einsum(
        "rcl,rol->co", taps, grad_mixed, preferred_element_type=jnp.float32
    ).reshape(KERNEL_TAPS, hid, hid)
    wide_grad = extended(grad_mixed, border, pairs)
    back_taps = shifted_taps(wide_grad, wide_ids, own_ids, back_offsets, border)
    kernel_back = jnp.transpose(w_cv, (0, 2, 1)).reshape(KERNEL_TAPS * hid, hid)
    grad_hidden1 = jnp.einsum(
        "oc,rol->rcl", kernel_back, back_taps, preferred_element_type=jnp.float32
    )
    grad_normed1 = gelu_back(normed1, grad_hidden1)
    grad_norm1_gain = jnp.sum(grad_normed1 * unit1, axis=(0, 2))
    grad_norm1_shift = jnp.sum(grad_normed1, axis=(0, 2))
    grad_inner = normalize_back(grad_normed1, unit1, scale1, g1).astype(jnp.bfloat16)
    grad_b_inner = jnp.sum(grad_inner.astype(jnp.float32), axis=(0, 2))
    grad_w_inner = jnp.einsum(
        "rdl,rhl->dh", hidden0, grad_inner, preferred_element_type=jnp.float32
    )
    grad_hidden0 = jnp.einsum("dh,rhl->rdl", w_in, grad_inner, preferred_element_type=jnp.float32)
    grad_normed0 = gelu_back(normed0, grad_hidden0)
    grad_norm0_gain = jnp.sum(grad_normed0 * unit0, axis=(0, 2))
    grad_norm0_shift = jnp.sum(grad_normed0, axis=(0, 2))
    input_grad = (cot.astype(jnp.float32) + normalize_back(grad_normed0, unit0, scale0, g0)).astype(
        jnp.bfloat16
    )
    output = to_channels(output, nch, q_count, rows)
    input_grad = to_channels(input_grad, nch, q_count, rows)
    grads = [
        grad_norm0_gain,
        grad_norm0_shift,
        grad_w_inner,
        grad_b_inner,
        grad_norm1_gain,
        grad_norm1_shift,
        grad_w_conv.transpose(1, 0, 2),
        grad_b_conv,
        grad_norm2_gain,
        grad_norm2_shift,
        grad_w_outer,
        grad_b_outer,
    ]
    flat = [g.reshape(nch, -1) for g in grads]
    sizes = [f.shape[1] for f in flat]
    stack = jnp.concatenate(flat, axis=1)
    total = stack.shape[1]
    lanes = 128
    spread = seqs * batches * 8 * lanes
    padded = -(-total // spread) * spread
    if padded != total:
        stack = jnp.pad(stack, ((0, 0), (0, padded - total)))
    stack = stack.reshape(nch, padded // lanes, lanes)
    stack = lax.psum_scatter(stack, "seq", scatter_dimension=1, tiled=True)
    stack = lax.psum_scatter(stack, "batch", scatter_dimension=1, tiled=True)
    stack = lax.psum_scatter(stack, "ch", scatter_dimension=0, tiled=True)
    stack = lax.all_gather(stack, ("seq", "batch"), axis=1, tiled=True).reshape(padded)[:total]
    shard_shapes = [
        norm0_gain.shape,
        norm0_shift.shape,
        w_inner.shape,
        b_inner.shape,
        norm1_gain.shape,
        norm1_shift.shape,
        (hloc, KERNEL_TAPS, hid),
        b_conv.shape,
        norm2_gain.shape,
        norm2_shift.shape,
        w_outer.shape,
        b_outer.shape,
    ]
    outs = []
    cut = 0
    for n, shape in zip(sizes, shard_shapes):
        outs.append(stack[cut : cut + n].reshape(shape))
        cut += n
    outs[6] = outs[6].transpose(1, 0, 2)
    return (output, input_grad, *outs)


def solution(mesh):
    return jax.shard_map(
        local,
        mesh=mesh,
        in_specs=(
            P("batch", "ch", "seq"),
            P("batch", "seq"),
            P("ch"),
            P("ch"),
            P("ch", None),
            P("ch"),
            P("ch"),
            P("ch"),
            P(None, "ch", None),
            P("ch"),
            P("ch"),
            P("ch"),
            P("ch", None),
            P("ch"),
            P("batch", "ch", "seq"),
        ),
        out_specs=(
            P("batch", "ch", "seq"),
            P("batch", "ch", "seq"),
            P("ch"),
            P("ch"),
            P("ch", None),
            P("ch"),
            P("ch"),
            P("ch"),
            P(None, "ch", None),
            P("ch"),
            P("ch"),
            P("ch"),
            P("ch", None),
            P("ch"),
        ),
        check_vma=False,
    )
```

profile of v0, /device:TPU:0, one launch (start us, length us, event | category | flops | bytes accessed | tf_op | source)
XLA Modules:
  0.0 816.1 jit_solution(5555885793643184578)
XLA Ops:
  10.0 1.8 reshape.1466
  13.4 5.3 all-to-all-start
  22.4 49.7 %all-gather.1 = f32[4,1,1920]{2,1,0:T(1,128)S(1)} all-gather(f32[1,1,1920]{2,1,0:T(1,128)S(1)} %reshape.1500), channel_id=2, replica_groups=mesh['batch'=4,'seq'=2,'ch'=4] {'ch'}, dimensions={0}, use_global_device_ids=true | all-gather | bytes 38400 | tf_op jit(solution)/shard_map/all_gather | solution.py:131
  73.7 4.8 all-to-all-start.2
  81.5 14.8 %fusion.6 = bf16[1,1280,1,1,1,1,1024]{6,1,5,4,3,2,0:T(8,128)(2,1)} fusion(f32[1,1280,1,1,1,1,1024]{6,1,5,4,3,2,0:T(8,128)S(1)} %bitcast.270, f32[1280]{0:T(1024)S(1)} %add.153, f32[1280]{0:T(1024)S(1)} %mul.431, f32[1024]{0:T(1024)S(1)} %add_rsqrt_fusion.2, f32[1024]{0:T(1024)S(1)} %broadcast_multiply_fusion.8), kind=kLoop, calls=%fused_computation.11 | loop fusion | flops 90439680 | bytes 7882752 | tf_op jit(solution)/shard_map/convert_element_type | solution.py:164
  96.3 48.7 %all-gather.5.cloned.1.call-done = bf16[4,7200,128]{2,1,0:T(8,128)(2,1)} async-done(((bf16[1,7200,128]{2,1,0:T(8,128)(2,1)}), bf16[4,7200,128]{2,1,0:T(8,128)(2,1)}) %all-gather.5.cloned.1.call-update) | async-done | bytes 7372816 | tf_op jit(solution)/shard_map/all_gather | solution.py:140
  145.0 26.1 %copy.86 = bf16[1,4,7200,128]{3,1,2,0:T(4,128)(2,1)S(1)} copy(bf16[1,4,7200,128]{3,2,1,0:T(8,128)(2,1)} %bitcast.283) | data formatting | bytes 14745600
  171.1 3.0 copy-done.6
  174.0 2.0 fusion.110
  176.1 2.3 reshape.1470
  178.4 4.5 fusion.72
  183.5 7.3 multiply_convert_fusion.1
  191.8 1.9 collective-permute-start.1
  193.8 2.7 convert_reduce_fusion.3
  196.5 5.9 copy.61
  202.4 3.6 slice.212
  206.6 2.4 copy.60
  208.9 4.1 reshape.1474
  214.3 7.9 copy.66
  222.2 2.9 fusion.90
  226.6 8.0 constant_dynamic-update-slice_fusion
  237.5 9.6 %copy.69 = bf16[1,3200,1024]{2,1,0:T(8,128)(2,1)} copy(bf16[1,3200,1024]{1,2,0:T(8,128)(2,1)} %fusion.97) | data formatting | bytes 13107200 | tf_op jit(solution)/shard_map/concatenate | solution.py:63
  247.0 9.1 %fusion.74 = (f32[1024]{0:T(1024)S(1)}, f32[1024,640]{1,0:T(8,128)S(1)}) fusion(f32[640]{0:T(1024)S(1)} %add.163, bf16[3200,640]{1,0:T(8,128)(2,1)} %bitcast.279, bf16[1,3200,1024]{1,2,0:T(8,128)(2,1)} %fusion.97), kind=kOutput, calls=%fused_computation.146 | convolution fusion | flops 4195613696 | bytes 13277696 | tf_op jit(solution)/shard_map/co,rcl->rol/dot_general | solution.py:174
  256.7 11.8 %fusion.105 = f32[640,1280]{1,0:T(8,128)} fusion(bf16[1280,1024]{1,0:T(8,128)(2,1)} %bitcast.15, f32[640]{0:T(1024)S(1)} %add.167, f32[640]{0:T(1024)S(1)} %mul.451, f32[1024]{0:T(1024)S(1)} %add_rsqrt_fusion, f32[1024]{0:T(1024)S(1)} %broadcast_multiply_fusion.4, f32[640]{0:T(1024)S(1)} %add.163, f32[1024,640]{1,0:T(8,128)S(1)} %get-tuple-element.121), kind=kOutput, calls=%fused_computation.218 | convolution fusion | flops 1723596800 | bytes 8535552 | tf_op jit(solution)/shard_map/rhl,rdl->hd/dot_general | solution.py:182
  268.6 12.4 %fusion.50 = (f32[640]{0:T(1024)S(1)}, f32[1024]{0:T(1024)S(1)}, f32[1024]{0:T(1024)S(1)}, f32[640]{0:T(1024)S(1)}, f32[1,640,1024]{1,2,0:T(8,128)}) fusion(f32[1024]{0:T(1024)S(1)} %add_rsqrt_fusion, f32[1024]{0:T(1024)S(1)} %broadcast_multiply_fusion.4, f32[640]{0:T(1024)S(1)} %add.163, f32[1024,640]{1,0:T(8,128)S(1)} %get-tuple-element.121, ...), kind=kOutput, calls=%fused_computation.93 | convolution fusion | flops 1732113152 | bytes 9531904 | tf_op jit(solution)/shard_map/hd,rdl->rhl/dot_general | solution.py:183
  281.1 3.1 convert_reduce_fusion.1
  284.3 5.2 reshape.1491
  289.5 3.0 collective-permute-start.5
  293.9 7.6 convolution_bitcast_fusion
  301.4 9.7 %copy.71 = f32[640,5,640]{2,1,0:T(8,128)} copy(f32[640,5,640]{2,0,1:T(8,128)S(1)} %convolution_bitcast_fusion) | data formatting | bytes 16384000 | tf_op jit(solution)/shard_map/transpose | solution.py:222
  311.2 12.0 %reshape.1487 = f32[4,512000]{1,0:T(4,128)} reshape(f32[640,5,640]{2,1,0:T(8,128)} %copy.71) | data formatting | bytes 16384000 | tf_op jit(solution)/shard_map/reshape | solution.py:229
  326.9 13.5 %fusion.56 = (f32[640]{0:T(1024)S(1)}, f32[1024]{0:T(1024)S(1)}, f32[1024]{0:T(1024)S(1)}, f32[640]{0:T(1024)S(1)}, f32[1,640,1024]{1,2,0:T(8,128)}) fusion(f32[1024]{0:T(1024)S(1)} %add_rsqrt_fusion.1, f32[1024]{0:T(1024)S(1)} %broadcast_multiply_fusion.5, f32[640]{0:T(1024)S(1)} %add.156, f32[1024,640]{1,0:T(8,128)S(1)} %copy-done.2, f32[640]{0:T(1024)S(1)} %mul.441, ...), kind=kOutput, calls=%fused_computation.104 | convolution fusion | flops 4248695808 | bytes 15921664 | tf_op jit(solution)/shard_map/oc,rol->rcl/dot_general | solution.py:195
  340.5 3.3 convert_reduce_fusion.2
  343.9 6.0 fusion.57
  349.9 3.5 reshape.1482
  353.4 19.2 %multiply_reduce_fusion = (f32[1280]{0:T(1024)S(1)}, f32[1024]{0:T(1024)S(1)}, f32[1024]{0:T(1024)S(1)}, f32[1280]{0:T(1024)S(1)}, f32[1,1280,1024]{1,2,0:T(8,128)}) fusion(f32[1,1280,1024]{1,2,0:T(8,128)} %copy.61, f32[1024]{0:T(1024)S(1)} %copy-done.15, f32[1024]{0:T(1024)S(1)} %copy-done.17, f32[1280]{0:T(1024)S(1)} %copy-done.13, ...), kind=kOutput, calls=%fused_computation.24 | convolution fusion | flops 1785196032 | bytes 13471744 | tf_op jit(solution)/shard_map/dh,rhl->rdl/dot_general | solution.py:206
  375.6 1.8 constant_dynamic-update-slice_fusion.2
  381.6 43.2 %dynamic-update-slice.6 = f32[4,923520]{1,0:T(4,128)} dynamic-update-slice(f32[4,923520]{1,0:T(4,128)} %dynamic-update-slice.5, f32[4,512000]{1,0:T(4,128)} %reshape.1487, s32[]{} %constant.29, s32[]{} %constant.35) | dynamic-update-slice | bytes 16384004
  426.2 1.7 dynamic-update-slice.8
  429.4 17.2 %dynamic-update-slice.10 = f32[4,923520]{1,0:T(4,128)} dynamic-update-slice(f32[4,923520]{1,0:T(4,128)} %dynamic-update-slice.9, f32[4,204800]{1,0:T(4,128)S(1)} %copy-done.7, s32[]{} %constant.29, s32[]{} %constant.146) | dynamic-update-slice | bytes 6553604
  448.0 12.8 %pad_bitcast_fusion = f32[1,4,7232,128]{3,1,2,0:T(4,128)} fusion(f32[4,923520]{1,0:T(4,128)} %dynamic-update-slice.11), kind=kLoop, calls=%fused_computation.1 | loop fusion | bytes 29587456
  460.8 11.4 %copy.85 = f32[1,4,7232,128]{3,2,1,0:T(8,128)} copy(f32[1,4,7232,128]{3,1,2,0:T(4,128)} %pad_bitcast_fusion) | data formatting | bytes 29622272
  472.2 24.9 %reduce-scatter.6.cloned.1.call-done = f32[4,3616,128]{2,1,0:T(8,128)} async-done(((f32[4,7232,128]{2,1,0:T(8,128)}), f32[4,3616,128]{2,1,0:T(8,128)}) %reduce-scatter.6.cloned.1.call-update) | async-done | bytes 7405584 | tf_op jit(solution)/shard_map/reduce_scatter | solution.py:239
  497.2 132.5 %reduce-scatter.8.cloned.1.call-done = f32[4,904,128]{2,1,0:T(8,128)} async-done(((f32[4,3616,128]{2,1,0:T(8,128)}), f32[4,904,128]{2,1,0:T(8,128)}) %reduce-scatter.8.cloned.1.call-update) | async-done | bytes 1851408 | tf_op jit(solution)/shard_map/reduce_scatter | solution.py:240
  629.7 37.5 %reduce-scatter.10.cloned.1.call-done = f32[1,904,128]{2,1,0:T(8,128)} async-done(((f32[4,904,128]{2,1,0:T(8,128)}), f32[1,904,128]{2,1,0:T(8,128)}) %reduce-scatter.10.cloned.1.call-update) | async-done | bytes 462864
  667.3 11.7 %fusion.12 = bf16[1,1280,1024]{1,2,0:T(8,128)(2,1)} fusion(f32[1,1280,1024]{1,2,0:T(8,128)} %copy.61, bf16[640,1280]{1,0:T(8,128)(2,1)} %reshape.1474, f32[1280]{0:T(1024)S(1)} %add.171, f32[640]{0:T(1024)S(1)} %add.167, f32[640]{0:T(1024)S(1)} %mul.451, f32[1024]{0:T(1024)S(1)} %add_rsqrt_fusion, f32[1024]{0:T(1024)S(1)} %broadcast_multiply_fusion.4, ...), kind=kOutput, calls=%fused_computation.18 | convolution fusion | flops 1727528960 | bytes 12145152 | tf_op jit(solution)/shard_map/hd,rhl->rdl/dot_general | solution.py:179
  679.0 11.6 %copy.62 = bf16[1,1280,1024]{2,0,1:T(2,128)(2,1)} copy(bf16[1,1280,1024]{1,2,0:T(8,128)(2,1)} %fusion.12) | data formatting | bytes 5242880 | tf_op jit(solution)/shard_map/convert_element_type | solution.py:180
  691.1 15.6 %reduce.29 = bf16[1280,1024]{1,0:T(8,128)(2,1)S(1)} reduce(bf16[1280,1,1024]{2,1,0:T(2,128)(2,1)} %bitcast.274, bf16[]{:T(256)} %broadcast.2394), dimensions={1}, to_apply=%bitcast.237.reduce_sub_computation | reduce | bytes 5242882
  706.7 3.1 reshape.1509
  709.9 4.6 all-to-all-start.1
  714.4 4.9 copy.67
  719.4 6.4 add_convert_fusion
  725.8 8.3 %copy.68 = bf16[1,1280,1024]{2,0,1:T(2,128)(2,1)} copy(bf16[1,1280,1024]{1,2,0:T(8,128)(2,1)S(1)} %add_convert_fusion) | data formatting | bytes 5242880 | tf_op jit(solution)/shard_map/convert_element_type | solution.py:210
  734.0 15.6 %reduce.30 = bf16[1280,1024]{1,0:T(8,128)(2,1)S(1)} reduce(bf16[1280,1,1024]{2,1,0:T(2,128)(2,1)} %bitcast.275, bf16[]{:T(256)} %broadcast.2394), dimensions={1}, to_apply=%bitcast.239.reduce_sub_computation | reduce | bytes 5242882
  749.6 3.2 reshape.1511
  752.8 4.3 all-to-all-start.3
  757.1 5.5 reshape.1510
  762.7 5.0 copy.77
  767.7 19.7 %all-to-all-done.3 = bf16[4,2,163840]{2,1,0:T(2,128)(2,1)S(1)} async-done(((bf16[4,2,163840]{2,1,0:T(2,128)(2,1)}), bf16[4,2,163840]{2,1,0:T(2,128)(2,1)S(1)}, u32[]{:S(2)}, u32[]{:S(2)}) %all-to-all-start.3) | async-done | bytes 2621472 | tf_op jit(solution)/shard_map/all_to_all | solution.py:75
  787.3 3.8 reshape.1512
  791.2 5.0 copy.78
  796.2 2.3 slice_bitcast_fusion
  800.1 1.9 slice.231
  805.2 2.4 reshape.1494
  (157 shorter events, 45.0 us)
Async XLA Ops:
  7.2 137.8 %all-gather.5.cloned.1.call-start = ((), (), s32[]{:S(2)}) async-start(), calls=%async_computation.7 | async-start | bytes 9216000 | tf_op jit(solution)/shard_map/all_gather | solution.py:140
  13.2 9.0 %copy-start.22 = (f32[320]{0:T(512)S(1)}, f32[320]{0:T(512)}, u32[]{:S(2)}) copy-start(f32[320]{0:T(512)} %param.17) | copy-start | bytes 3844
  13.3 9.0 %copy-start.23 = (f32[320]{0:T(512)S(1)}, f32[320]{0:T(512)}, u32[]{:S(2)}) copy-start(f32[320]{0:T(512)} %param.18) | copy-start | bytes 3844
  13.3 9.0 %copy-start.24 = (f32[320]{0:T(512)S(1)}, f32[320]{0:T(512)}, u32[]{:S(2)}) copy-start(f32[320]{0:T(512)} %param.28) | copy-start | bytes 3844
  13.3 9.0 %copy-start.25 = (f32[160]{0:T(256)S(1)}, f32[160]{0:T(256)}, u32[]{:S(2)}) copy-start(f32[160]{0:T(256)} %param.20) | copy-start | bytes 1924
  13.3 9.0 %copy-start.26 = (f32[160]{0:T(256)S(1)}, f32[160]{0:T(256)}, u32[]{:S(2)}) copy-start(f32[160]{0:T(256)} %param.21) | copy-start | bytes 1924
  13.3 9.0 %copy-start.27 = (f32[160]{0:T(256)S(1)}, f32[160]{0:T(256)}, u32[]{:S(2)}) copy-start(f32[160]{0:T(256)} %param.22) | copy-start | bytes 1924
  13.3 9.0 %copy-start.28 = (f32[160]{0:T(256)S(1)}, f32[160]{0:T(256)}, u32[]{:S(2)}) copy-start(f32[160]{0:T(256)} %param.24) | copy-start | bytes 1924
  13.3 9.0 %copy-start.29 = (f32[160]{0:T(256)S(1)}, f32[160]{0:T(256)}, u32[]{:S(2)}) copy-start(f32[160]{0:T(256)} %param.25) | copy-start | bytes 1924
  13.3 9.0 %copy-start.30 = (f32[160]{0:T(256)S(1)}, f32[160]{0:T(256)}, u32[]{:S(2)}) copy-start(f32[160]{0:T(256)} %param.26) | copy-start | bytes 1924
  13.4 60.4 %all-to-all-start = ((bf16[4,320,1024]{2,1,0:T(8,128)(2,1)}), bf16[4,320,1024]{2,1,0:T(8,128)(2,1)S(1)}, u32[]{:S(2)}, u32[]{:S(2)}) async-start(bf16[4,320,1024]{2,1,0:T(8,128)(2,1)} %param.15), calls=%async_computation | async-start | bytes 5242880 | tf_op jit(solution)/shard_map/all_to_all | solution.py:71
  19.5 54.1 %collective-permute-start = (s32[1,64]{1,0:T(1,128)S(1)}, s32[1,64]{1,0:T(1,128)S(1)}, u32[]{:S(2)}, u32[]{:S(2)}) collective-permute-start(s32[1,64]{1,0:T(1,128)S(1)} %get-tuple-element.116), channel_id=1, source_target_pairs={{0,4},{1,5},{2,6},{3,7},{8,12},{9,13},{10,14},{11,15},{16,20},{17,... | collective-permute-start | bytes 776 | tf_op jit(solution)/shard_map/ppermute | solution.py:50
  20.9 52.6 %collective-permute-start.2 = (s32[1,64]{1,0:T(1,128)S(1)}, s32[1,64]{1,0:T(1,128)S(1)}, u32[]{:S(2)}, u32[]{:S(2)}) collective-permute-start(s32[1,64]{1,0:T(1,128)S(1)} %get-tuple-element.117), channel_id=1, source_target_pairs={{4,0},{5,1},{6,2},{7,3},{12,8},{13,9},{14,10},{15,11},{20,16},{21,... | collective-permute-start | bytes 776 | tf_op jit(solution)/shard_map/ppermute | solution.py:51
  73.1 7.3 copy-start.12
  73.6 6.9 copy-start.18
  73.7 120.1 %all-to-all-start.2 = ((bf16[4,320,1024]{2,1,0:T(8,128)(2,1)}), bf16[4,320,1024]{2,1,0:T(8,128)(2,1)}, u32[]{:S(2)}, u32[]{:S(2)}) async-start(bf16[4,320,1024]{2,1,0:T(8,128)(2,1)} %param.29), calls=%async_computation.2 | async-start | bytes 5242880 | tf_op jit(solution)/shard_map/all_to_all | solution.py:71
  78.5 418.6 %reduce-scatter.6.cloned.1.call-start = ((), (), s32[]{:S(2)}) async-start(), calls=%async_computation.8 | async-start | bytes 22216704 | tf_op jit(solution)/shard_map/reduce_scatter | solution.py:239
  79.2 2.3 copy-start
  79.6 16.6 %copy-start.14 = (f32[1024]{0:T(1024)}, f32[1024]{0:T(1024)S(1)}, u32[]{:S(2)}) copy-start(f32[1024]{0:T(1024)S(1)} %broadcast_multiply_fusion.8) | copy-start | bytes 12292
  80.4 15.9 %copy-start.16 = (f32[1024]{0:T(1024)}, f32[1024]{0:T(1024)S(1)}, u32[]{:S(2)}) copy-start(f32[1024]{0:T(1024)S(1)} %add_rsqrt_fusion.2) | copy-start | bytes 12292
  171.0 3.0 copy-start.6
  182.9 43.6 %copy-start.1 = (f32[1024,640]{1,0:T(8,128)}, f32[1024,640]{1,0:T(8,128)S(1)}, u32[]{:S(2)}) copy-start(f32[1024,640]{1,0:T(8,128)S(1)} %get-tuple-element.119) | copy-start | bytes 7864324
  190.8 1.1 copy-start.4
  191.8 30.4 %collective-permute-start.1 = (bf16[1,640,64]{1,2,0:T(8,128)(2,1)S(1)}, bf16[1,640,64]{1,2,0:T(8,128)(2,1)S(1)}, u32[]{:S(2)}, u32[]{:S(2)}) collective-permute-start(bf16[1,640,64]{1,2,0:T(8,128)(2,1)S(1)} %get-tuple-element.106), channel_id=1, source_target_pairs={{0,4},{1,5},{2,6},{3,7},{8,12},{9,13},{10,14},{11,15},{16,20},{17,... | collective-permute-start | bytes 245768 | tf_op jit(solution)/shard_map/ppermute | solution.py:50
  213.1 21.5 %collective-permute-start.3 = (bf16[1,640,64]{1,2,0:T(8,128)(2,1)S(1)}, bf16[1,640,64]{1,2,0:T(8,128)(2,1)S(1)}, u32[]{:S(2)}, u32[]{:S(2)}) collective-permute-start(bf16[1,640,64]{1,2,0:T(8,128)(2,1)S(1)} %get-tuple-element.105), channel_id=1, source_target_pairs={{4,0},{5,1},{6,2},{7,3},{12,8},{13,9},{14,10},{15,11},{20,16},{21,... | collective-permute-start | bytes 245768 | tf_op jit(solution)/shard_map/ppermute | solution.py:51
  222.2 2.9 copy-start.5
  256.2 12.4 %copy-start.8 = (f32[1024,640]{1,0:T(8,128)}, f32[1024,640]{1,0:T(8,128)S(1)}, u32[]{:S(2)}) copy-start(f32[1024,640]{1,0:T(8,128)S(1)} %get-tuple-element.121) | copy-start | bytes 7864324
  256.7 11.8 %copy-start.11 = (bf16[640,1280]{1,0:T(8,128)(2,1)S(1)}, bf16[640,1280]{1,0:T(8,128)(2,1)}, u32[]{:S(2)}) copy-start(bf16[640,1280]{1,0:T(8,128)(2,1)} %reshape.1474) | copy-start | bytes 4915204
  289.5 34.6 %collective-permute-start.5 = (bf16[1,640,64]{1,2,0:T(8,128)(2,1)S(1)}, bf16[1,640,64]{1,2,0:T(8,128)(2,1)S(1)}, u32[]{:S(2)}, u32[]{:S(2)}) collective-permute-start(bf16[1,640,64]{1,2,0:T(8,128)(2,1)S(1)} %get-tuple-element.103), channel_id=1, source_target_pairs={{0,4},{1,5},{2,6},{3,7},{8,12},{9,13},{10,14},{11,15},{16,20},{17,... | collective-permute-start | bytes 245768 | tf_op jit(solution)/shard_map/ppermute | solution.py:50
  292.6 30.6 %collective-permute-start.4 = (bf16[1,640,64]{1,2,0:T(8,128)(2,1)S(1)}, bf16[1,640,64]{1,2,0:T(8,128)(2,1)S(1)}, u32[]{:S(2)}, u32[]{:S(2)}) collective-permute-start(bf16[1,640,64]{1,2,0:T(8,128)(2,1)S(1)} %get-tuple-element.104), channel_id=1, source_target_pairs={{4,0},{5,1},{6,2},{7,3},{12,8},{13,9},{14,10},{15,11},{20,16},{21,... | collective-permute-start | bytes 245768 | tf_op jit(solution)/shard_map/ppermute | solution.py:51
  323.9 2.2 copy-start.10
  324.1 2.8 copy-start.2
  326.9 13.6 %copy-start.3 = (f32[1024,640]{1,0:T(8,128)S(1)}, f32[1024,640]{1,0:T(8,128)}, u32[]{:S(2)}) copy-start(f32[1024,640]{1,0:T(8,128)} %copy-done.1) | copy-start | bytes 7864324
  349.9 3.5 copy-start.13
  349.9 3.5 copy-start.15
  349.9 3.5 copy-start.17
  349.9 3.5 copy-start.19
  381.6 47.8 %copy-start.7 = (f32[4,204800]{1,0:T(4,128)S(1)}, f32[4,204800]{1,0:T(4,128)}, u32[]{:S(2)}) copy-start(f32[4,204800]{1,0:T(4,128)} %reshape.1491) | copy-start | bytes 9830404
  429.4 17.3 %copy-start.21 = (f32[4,320]{1,0:T(4,128)S(1)}, f32[4,320]{1,0:T(4,128)}, u32[]{:S(2)}) copy-start(f32[4,320]{1,0:T(4,128)} %convert_reduce_fusion.3) | copy-start | bytes 15364
  472.1 157.5 %reduce-scatter.8.cloned.1.call-start = ((), (), s32[]{:S(2)}) async-start(), calls=%async_computation.9 | async-start | bytes 9256960 | tf_op jit(solution)/shard_map/reduce_scatter | solution.py:240
  497.1 170.1 %copy-start.20 = (f32[4,320]{1,0:T(4,128)S(1)}, f32[4,320]{1,0:T(4,128)}, u32[]{:S(2)}) copy-start(f32[4,320]{1,0:T(4,128)} %get-tuple-element.114) | copy-start | bytes 15364
  497.1 170.2 %copy-start.9 = (f32[1024,640]{1,0:T(8,128)S(1)}, f32[1024,640]{1,0:T(8,128)}, u32[]{:S(2)}) copy-start(f32[1024,640]{1,0:T(8,128)} %copy-done.8) | copy-start | bytes 7864324
  497.2 170.1 %reduce-scatter.10.cloned.1.call-start = ((), (), s32[]{:S(2)}) async-start(), calls=%async_computation.11 | async-start | bytes 2314240
  629.7 166.5 %all-gather.7.cloned.1.call-start = ((), (), s32[]{:S(2)}) async-start(), calls=%async_computation.10 | async-start | bytes 4165632 | tf_op jit(solution)/shard_map/all_gather | solution.py:242
  709.9 43.0 %all-to-all-start.1 = ((bf16[4,2,163840]{2,1,0:T(2,128)(2,1)}), bf16[4,2,163840]{2,1,0:T(2,128)(2,1)}, u32[]{:S(2)}, u32[]{:S(2)}) async-start(bf16[4,2,163840]{2,1,0:T(2,128)(2,1)} %reshape.1509), calls=%async_computation.1 | async-start | bytes 5242880 | tf_op jit(solution)/shard_map/all_to_all | solution.py:75
  752.8 34.5 %all-to-all-start.3 = ((bf16[4,2,163840]{2,1,0:T(2,128)(2,1)}), bf16[4,2,163840]{2,1,0:T(2,128)(2,1)S(1)}, u32[]{:S(2)}, u32[]{:S(2)}) async-start(bf16[4,2,163840]{2,1,0:T(2,128)(2,1)} %reshape.1511), calls=%async_computation.3 | async-start | bytes 5242880 | tf_op jit(solution)/shard_map/all_to_all | solution.py:75
Sparse Core Ops, SparseCore 0:
  13.4 131.5 all-gather.4
  472.3 24.8 reduce-scatter.5
  499.5 130.0 reduce-scatter.7
  632.5 34.6 reduce-scatter.9
  668.7 42.8 all-gather.6
where the time goes:
time: 824 us; the launch traced here: 816 us
  local copies, waits for them, and re-layouts  273 us (33%)
  waiting for transfers between devices  263 us (32%)
  matrix products  95.8 us (12%)
  other arithmetic  90.6 us (11%)
  blocking collectives  49.7 us (6%)
  starting transfers between devices  29.4 us (4%)
  between operations  14.6 us (2%)
    unnamed x88, local copies, waits for them, and re-layouts  160 us
    reduce_scatter x1, waiting for transfers between devices, local(): stack = lax.psum_scatter(stack, 'batch', scatter_dimension=1, tiled=True)  132 us
    all_gather x1, blocking collectives, local(): lax.all_gather(jnp.concatenate(smalls), 'ch', axis=0, tiled=False)  49.7 us
    all_gather x1, waiting for transfers between devices, local(): lax.all_gather(packed.reshape(1, -1, 128), 'ch', axis=0, tiled=True)  48.7 us
    unnamed x10, other arithmetic  46 us
    unnamed x6, waiting for transfers between devices  37.6 us
    reduce_scatter x1, waiting for transfers between devices, local(): stack = lax.psum_scatter(stack, 'seq', scatter_dimension=1, tiled=True)  24.9 us
    reshape x11, local copies, waits for them, and re-layouts, local(): flat = [g.reshape(nch, -1) for g in grads]  21.3 us
  transfers between devices with their start and end apart: 15, of which 5 were waited for; matrix products, arithmetic and copies ran while one was open for 28% of the time, Pallas kernels for 0%

commit v1 on v0

--- a/solution.py
+++ b/solution.py
@@ -72,7 +72,9 @@
 
 
 def to_channels(x, nch, q_count, rows):
-    x = lax.all_to_all(x, "ch", 1, 0, tiled=True)
+    x = jnp.concatenate(
+        lax.all_to_all(jnp.stack(jnp.split(x, lax.axis_size("ch"), axis=1)), "ch", 0, 0), axis=0
+    )
     if q_count > 1:
         _, width, part = x.shape
         x = (

time: 824 us -> 785 us (0.953)
  local copies, waits for them, and re-layouts: 273 us -> 240 us
  other arithmetic: 90.6 us -> 61.2 us
  waiting for transfers between devices: 263 us -> 288 us
    unnamed x10 -> x8, other arithmetic: 46 us -> 14.9 us
    all_to_all x2, waiting for transfers between devices: 19.7 us -> 49.8 us  [to_channels(): lax.all_to_all(jnp.stack(jnp.split(x, lax.axis_size('ch'), axis=1)), 'ch'...]
    unnamed x88 -> x87, local copies, waits for them, and re-layouts: 160 us -> 139 us
    convert_element_type x2 -> x0, local copies, waits for them, and re-layouts: 19.9 us -> none  [the longest x1 11.6 us: local(): output = (residual + branch + b_out[:, None]).astype(jnp.bfloat16)]
  transfers between devices with their start and end apart: 15 -> 15, of which waited for: 5 -> 6; matrix products, arithmetic and copies ran while one was open for 28% -> 21% of each run, Pallas kernels for 0% -> 0%
where the time goes in v1:
time: 785 us; the launch traced here: 778 us
  waiting for transfers between devices  288 us (37%)
  local copies, waits for them, and re-layouts  240 us (31%)
  matrix products  95 us (12%)
  other arithmetic  61.2 us (8%)
  blocking collectives  49.7 us (6%)
  starting transfers between devices  28.8 us (4%)
  between operations  14.9 us (2%)
    unnamed x87, local copies, waits for them, and re-layouts  139 us
    reduce_scatter x1, waiting for transfers between devices, local(): stack = lax.psum_scatter(stack, 'batch', scatter_dimension=1, tiled=True)  132 us
    all_to_all x2, waiting for transfers between devices, to_channels(): lax.all_to_all(jnp.stack(jnp.split(x, lax.axis_size('ch'), axis=1)), 'ch'...  49.8 us
    all_gather x1, blocking collectives, local(): lax.all_gather(jnp.concatenate(smalls), 'ch', axis=0, tiled=False)  49.7 us
    all_gather x1, waiting for transfers between devices, local(): lax.all_gather(packed.reshape(1, -1, 128), 'ch', axis=0, tiled=True)  48.7 us
    unnamed x6, waiting for transfers between devices  32.5 us
    reduce_scatter x1, waiting for transfers between devices, local(): stack = lax.psum_scatter(stack, 'seq', scatter_dimension=1, tiled=True)  24.9 us
    reshape x11, local copies, waits for them, and re-layouts, local(): flat = [g.reshape(nch, -1) for g in grads]  21.3 us
  transfers between devices with their start and end apart: 15, of which 6 were waited for; matrix products, arithmetic and copies ran while one was open for 21% of the time, Pallas kernels for 0%

profile of v1, /device:TPU:0, one launch (start us, length us, event | category | flops | bytes accessed | tf_op | source)
XLA Modules:
  0.0 777.7 jit_solution(13455571146473707824)
XLA Ops:
  8.5 1.5 reshape.1467
  10.0 1.8 reshape.1466
  13.4 5.3 all-to-all-start
  22.4 49.7 %all-gather.1 = f32[4,1,1920]{2,1,0:T(1,128)S(1)} all-gather(f32[1,1,1920]{2,1,0:T(1,128)S(1)} %reshape.1502), channel_id=2, replica_groups=mesh['batch'=4,'seq'=2,'ch'=4] {'ch'}, dimensions={0}, use_global_device_ids=true | all-gather | bytes 38400 | tf_op jit(solution)/shard_map/all_gather | solution.py:133
  73.7 4.8 all-to-all-start.2
  81.5 14.8 %fusion.6 = bf16[1,1280,1,1,1,1,1024]{6,1,5,4,3,2,0:T(8,128)(2,1)} fusion(f32[1,1280,1,1,1,1,1024]{6,1,5,4,3,2,0:T(8,128)S(1)} %bitcast.282, f32[1280]{0:T(1024)S(1)} %add.153, f32[1280]{0:T(1024)S(1)} %mul.431, f32[1024]{0:T(1024)S(1)} %add_rsqrt_fusion.2, f32[1024]{0:T(1024)S(1)} %broadcast_multiply_fusion.8), kind=kLoop, calls=%fused_computation.11 | loop fusion | flops 90439680 | bytes 7882752 | tf_op jit(solution)/shard_map/convert_element_type | solution.py:166
  96.2 48.7 %all-gather.5.cloned.1.call-done = bf16[4,7200,128]{2,1,0:T(8,128)(2,1)} async-done(((bf16[1,7200,128]{2,1,0:T(8,128)(2,1)}), bf16[4,7200,128]{2,1,0:T(8,128)(2,1)}) %all-gather.5.cloned.1.call-update) | async-done | bytes 7372816 | tf_op jit(solution)/shard_map/all_gather | solution.py:142
  145.0 26.1 %copy.84 = bf16[1,4,7200,128]{3,1,2,0:T(4,128)(2,1)S(1)} copy(bf16[1,4,7200,128]{3,2,1,0:T(8,128)(2,1)} %bitcast.292) | data formatting | bytes 14745600
  171.1 3.0 copy-done.6
  174.0 2.0 fusion.110
  176.1 2.3 reshape.1470
  178.4 4.5 fusion.72
  183.5 7.3 multiply_convert_fusion.1
  191.8 1.9 collective-permute-start.1
  193.8 2.7 convert_reduce_fusion.3
  196.5 5.9 copy.61
  202.4 3.6 slice.212
  206.6 2.4 copy.60
  208.9 4.1 reshape.1474
  214.3 7.9 %copy.66 = bf16[5,640,640]{2,1,0:T(8,128)(2,1)} copy(bf16[5,640,640]{1,2,0:T(8,128)(2,1)} %bitcast.286) | data formatting | bytes 8192000 | tf_op jit(solution)/shard_map/transpose | solution.py:196
  222.2 2.9 fusion.90
  225.1 1.5 fusion.99
  226.6 8.0 %constant_dynamic-update-slice_fusion = bf16[1,3200,1024]{1,2,0:T(8,128)(2,1)} fusion(bf16[1,3200,1024]{1,2,0:T(8,128)(2,1)} %fusion.99, f32[640]{0:T(1024)S(1)} %add.160, f32[640]{0:T(1024)S(1)} %mul.441, f32[1024]{0:T(1024)S(1)} %add_rsqrt_fusion.1, f32[1024]{0:T(1024)S(1)} %broadcast_multiply_fusion.5, f32[640]{0:T(1024)S(1)} %add.156, ...), kind=kLoop, calls=%fused_computation.200 | loop fusion | flops 45875200 | bytes 3948032
  234.6 1.5 fusion.87
  237.5 9.6 %copy.69 = bf16[1,3200,1024]{2,1,0:T(8,128)(2,1)} copy(bf16[1,3200,1024]{1,2,0:T(8,128)(2,1)} %fusion.97) | data formatting | bytes 13107200 | tf_op jit(solution)/shard_map/concatenate | solution.py:63
  247.0 9.1 %fusion.74 = (f32[1024]{0:T(1024)S(1)}, f32[1024,640]{1,0:T(8,128)S(1)}) fusion(f32[640]{0:T(1024)S(1)} %add.163, bf16[3200,640]{1,0:T(8,128)(2,1)} %bitcast.287, bf16[1,3200,1024]{1,2,0:T(8,128)(2,1)} %fusion.97), kind=kOutput, calls=%fused_computation.148 | convolution fusion | flops 4195613696 | bytes 13277696 | tf_op jit(solution)/shard_map/co,rcl->rol/dot_general | solution.py:176
  256.7 11.8 %fusion.105 = f32[640,1280]{1,0:T(8,128)} fusion(bf16[1280,1024]{1,0:T(8,128)(2,1)} %bitcast.20, f32[640]{0:T(1024)S(1)} %add.167, f32[640]{0:T(1024)S(1)} %mul.451, f32[1024]{0:T(1024)S(1)} %add_rsqrt_fusion, f32[1024]{0:T(1024)S(1)} %broadcast_multiply_fusion.4, f32[640]{0:T(1024)S(1)} %add.163, f32[1024,640]{1,0:T(8,128)S(1)} %get-tuple-element.129), kind=kOutput, calls=%fused_computation.228 | convolution fusion | flops 1723596800 | bytes 8535552 | tf_op jit(solution)/shard_map/rhl,rdl->hd/dot_general | solution.py:184
  268.6 12.4 %fusion.50 = (f32[640]{0:T(1024)S(1)}, f32[1024]{0:T(1024)S(1)}, f32[1024]{0:T(1024)S(1)}, f32[640]{0:T(1024)S(1)}, f32[1,640,1024]{1,2,0:T(8,128)}) fusion(f32[1024]{0:T(1024)S(1)} %add_rsqrt_fusion, f32[1024]{0:T(1024)S(1)} %broadcast_multiply_fusion.4, f32[640]{0:T(1024)S(1)} %add.163, f32[1024,640]{1,0:T(8,128)S(1)} %get-tuple-element.129, ...), kind=kOutput, calls=%fused_computation.95 | convolution fusion | flops 1732113152 | bytes 9531904 | tf_op jit(solution)/shard_map/hd,rdl->rhl/dot_general | solution.py:185
  281.1 3.1 convert_reduce_fusion.1
  284.3 5.2 reshape.1493
  289.5 3.0 collective-permute-start.5
  293.9 7.6 convolution_bitcast_fusion
  301.5 9.7 %copy.71 = f32[640,5,640]{2,1,0:T(8,128)} copy(f32[640,5,640]{2,0,1:T(8,128)S(1)} %convolution_bitcast_fusion) | data formatting | bytes 16384000 | tf_op jit(solution)/shard_map/transpose | solution.py:224
  311.2 12.0 %reshape.1489 = f32[4,512000]{1,0:T(4,128)} reshape(f32[640,5,640]{2,1,0:T(8,128)} %copy.71) | data formatting | bytes 16384000 | tf_op jit(solution)/shard_map/reshape | solution.py:231
  326.9 13.5 %fusion.56 = (f32[640]{0:T(1024)S(1)}, f32[1024]{0:T(1024)S(1)}, f32[1024]{0:T(1024)S(1)}, f32[640]{0:T(1024)S(1)}, f32[1,640,1024]{1,2,0:T(8,128)}) fusion(f32[1024]{0:T(1024)S(1)} %add_rsqrt_fusion.1, f32[1024]{0:T(1024)S(1)} %broadcast_multiply_fusion.5, f32[640]{0:T(1024)S(1)} %add.156, f32[1024,640]{1,0:T(8,128)S(1)} %copy-done.2, f32[640]{0:T(1024)S(1)} %mul.441, ...), kind=kOutput, calls=%fused_computation.106 | convolution fusion | flops 4248695808 | bytes 15921664 | tf_op jit(solution)/shard_map/oc,rol->rcl/dot_general | solution.py:197
  340.5 3.3 convert_reduce_fusion.2
  343.9 6.0 fusion.57
  349.9 3.5 reshape.1484
  353.4 19.2 %multiply_reduce_fusion = (f32[1280]{0:T(1024)S(1)}, f32[1024]{0:T(1024)S(1)}, f32[1024]{0:T(1024)S(1)}, f32[1280]{0:T(1024)S(1)}, f32[1,1280,1024]{1,2,0:T(8,128)}) fusion(f32[1,1280,1024]{1,2,0:T(8,128)} %copy.61, f32[1024]{0:T(1024)S(1)} %copy-done.17, f32[1024]{0:T(1024)S(1)} %copy-done.19, f32[1280]{0:T(1024)S(1)} %copy-done.15, ...), kind=kOutput, calls=%fused_computation.24 | convolution fusion | flops 1785196032 | bytes 13471744 | tf_op jit(solution)/shard_map/dh,rhl->rdl/dot_general | solution.py:208
  374.1 1.5 dynamic-update-slice.1
  375.6 1.8 constant_dynamic-update-slice_fusion.2
  381.6 43.2 %dynamic-update-slice.6 = f32[4,923520]{1,0:T(4,128)} dynamic-update-slice(f32[4,923520]{1,0:T(4,128)} %dynamic-update-slice.5, f32[4,512000]{1,0:T(4,128)} %reshape.1489, s32[]{} %constant.29, s32[]{} %constant.35) | dynamic-update-slice | bytes 16384004
  426.2 1.6 dynamic-update-slice.8
  429.2 17.2 %dynamic-update-slice.10 = f32[4,923520]{1,0:T(4,128)} dynamic-update-slice(f32[4,923520]{1,0:T(4,128)} %dynamic-update-slice.9, f32[4,204800]{1,0:T(4,128)S(1)} %copy-done.7, s32[]{} %constant.29, s32[]{} %constant.146) | dynamic-update-slice | bytes 6553604
  447.9 12.8 %pad_bitcast_fusion = f32[1,4,7232,128]{3,1,2,0:T(4,128)} fusion(f32[4,923520]{1,0:T(4,128)} %dynamic-update-slice.11), kind=kLoop, calls=%fused_computation.1 | loop fusion | bytes 29587456
  460.6 11.4 %copy.83 = f32[1,4,7232,128]{3,2,1,0:T(8,128)} copy(f32[1,4,7232,128]{3,1,2,0:T(4,128)} %pad_bitcast_fusion) | data formatting | bytes 29622272
  472.0 24.9 %reduce-scatter.6.cloned.1.call-done = f32[4,3616,128]{2,1,0:T(8,128)} async-done(((f32[4,7232,128]{2,1,0:T(8,128)}), f32[4,3616,128]{2,1,0:T(8,128)}) %reduce-scatter.6.cloned.1.call-update) | async-done | bytes 7405584 | tf_op jit(solution)/shard_map/reduce_scatter | solution.py:241
  497.0 132.5 %reduce-scatter.8.cloned.1.call-done = f32[4,904,128]{2,1,0:T(8,128)} async-done(((f32[4,3616,128]{2,1,0:T(8,128)}), f32[4,904,128]{2,1,0:T(8,128)}) %reduce-scatter.8.cloned.1.call-update) | async-done | bytes 1851408 | tf_op jit(solution)/shard_map/reduce_scatter | solution.py:242
  629.7 5.1 copy.67
  634.7 32.4 %reduce-scatter.10.cloned.1.call-done = f32[1,904,128]{2,1,0:T(8,128)} async-done(((f32[4,904,128]{2,1,0:T(8,128)}), f32[1,904,128]{2,1,0:T(8,128)}) %reduce-scatter.10.cloned.1.call-update) | async-done | bytes 462864
  667.1 10.9 %fusion.12 = bf16[1,1280,1024]{1,2,0:T(8,128)(2,1)S(1)} fusion(f32[1,1280,1024]{1,2,0:T(8,128)} %copy.61, bf16[640,1280]{1,0:T(8,128)(2,1)} %reshape.1474, f32[1280]{0:T(1024)S(1)} %add.171, f32[640]{0:T(1024)S(1)} %add.167, f32[640]{0:T(1024)S(1)} %mul.451, f32[1024]{0:T(1024)S(1)} %add_rsqrt_fusion, f32[1024]{0:T(1024)S(1)} %broadcast_multiply_fusion.4, ...), kind=kOutput, calls=%fused_computation.18 | convolution fusion | flops 1727528960 | bytes 12145152 | tf_op jit(solution)/shard_map/hd,rhl->rdl/dot_general | solution.py:181
  679.7 2.7 copy.62
  682.4 4.6 all-to-all-start.1
  687.0 6.6 add_convert_fusion
  695.2 2.7 copy.68
  698.0 19.9 %all-to-all-done.1 = bf16[4,1,320,1024]{3,2,1,0:T(8,128)(2,1)} async-done(((bf16[4,1,320,1024]{3,2,1,0:T(8,128)(2,1)}), bf16[4,1,320,1024]{3,2,1,0:T(8,128)(2,1)}, u32[]{:S(2)}, u32[]{:S(2)}) %all-to-all-start.1) | async-done | bytes 2621472 | tf_op jit(solution)/shard_map/all_to_all | solution.py:76
  717.8 3.7 all-to-all-start.3
  721.5 29.9 %all-to-all-done.3 = bf16[4,1,320,1024]{3,2,1,0:T(8,128)(2,1)S(1)} async-done(((bf16[4,1,320,1024]{3,2,1,0:T(8,128)(2,1)}), bf16[4,1,320,1024]{3,2,1,0:T(8,128)(2,1)S(1)}, u32[]{:S(2)}, u32[]{:S(2)}) %all-to-all-start.3) | async-done | bytes 2621472 | tf_op jit(solution)/shard_map/all_to_all | solution.py:76
  751.4 3.2 slice_bitcast_fusion
  756.3 1.9 slice.231
  761.5 2.4 reshape.1496
  763.9 1.7 copy.72
  765.6 3.6 copy.108
  769.2 1.5 copy.109
  (158 shorter events, 40.1 us)
Async XLA Ops:
  7.2 137.8 %all-gather.5.cloned.1.call-start = ((), (), s32[]{:S(2)}) async-start(), calls=%async_computation.7 | async-start | bytes 9216000 | tf_op jit(solution)/shard_map/all_gather | solution.py:142
  13.2 9.0 %copy-start.24 = (f32[320]{0:T(512)S(1)}, f32[320]{0:T(512)}, u32[]{:S(2)}) copy-start(f32[320]{0:T(512)} %param.17) | copy-start | bytes 3844
  13.3 9.0 %copy-start.25 = (f32[320]{0:T(512)S(1)}, f32[320]{0:T(512)}, u32[]{:S(2)}) copy-start(f32[320]{0:T(512)} %param.18) | copy-start | bytes 3844
  13.3 9.0 %copy-start.26 = (f32[320]{0:T(512)S(1)}, f32[320]{0:T(512)}, u32[]{:S(2)}) copy-start(f32[320]{0:T(512)} %param.28) | copy-start | bytes 3844
  13.3 9.0 %copy-start.27 = (f32[160]{0:T(256)S(1)}, f32[160]{0:T(256)}, u32[]{:S(2)}) copy-start(f32[160]{0:T(256)} %param.20) | copy-start | bytes 1924
  13.3 9.0 %copy-start.28 = (f32[160]{0:T(256)S(1)}, f32[160]{0:T(256)}, u32[]{:S(2)}) copy-start(f32[160]{0:T(256)} %param.21) | copy-start | bytes 1924
  13.3 9.0 %copy-start.29 = (f32[160]{0:T(256)S(1)}, f32[160]{0:T(256)}, u32[]{:S(2)}) copy-start(f32[160]{0:T(256)} %param.22) | copy-start | bytes 1924
  13.3 9.0 %copy-start.30 = (f32[160]{0:T(256)S(1)}, f32[160]{0:T(256)}, u32[]{:S(2)}) copy-start(f32[160]{0:T(256)} %param.24) | copy-start | bytes 1924
  13.3 9.0 %copy-start.31 = (f32[160]{0:T(256)S(1)}, f32[160]{0:T(256)}, u32[]{:S(2)}) copy-start(f32[160]{0:T(256)} %param.25) | copy-start | bytes 1924
  13.3 9.0 %copy-start.32 = (f32[160]{0:T(256)S(1)}, f32[160]{0:T(256)}, u32[]{:S(2)}) copy-start(f32[160]{0:T(256)} %param.26) | copy-start | bytes 1924
  13.4 60.4 %all-to-all-start = ((bf16[4,320,1024]{2,1,0:T(8,128)(2,1)}), bf16[4,320,1024]{2,1,0:T(8,128)(2,1)S(1)}, u32[]{:S(2)}, u32[]{:S(2)}) async-start(bf16[4,320,1024]{2,1,0:T(8,128)(2,1)} %param.15), calls=%async_computation | async-start | bytes 5242880 | tf_op jit(solution)/shard_map/all_to_all | solution.py:71
  19.5 54.1 %collective-permute-start = (s32[1,64]{1,0:T(1,128)S(1)}, s32[1,64]{1,0:T(1,128)S(1)}, u32[]{:S(2)}, u32[]{:S(2)}) collective-permute-start(s32[1,64]{1,0:T(1,128)S(1)} %get-tuple-element.124), channel_id=1, source_target_pairs={{0,4},{1,5},{2,6},{3,7},{8,12},{9,13},{10,14},{11,15},{16,20},{17,... | collective-permute-start | bytes 776 | tf_op jit(solution)/shard_map/ppermute | solution.py:50
  20.9 52.6 %collective-permute-start.2 = (s32[1,64]{1,0:T(1,128)S(1)}, s32[1,64]{1,0:T(1,128)S(1)}, u32[]{:S(2)}, u32[]{:S(2)}) collective-permute-start(s32[1,64]{1,0:T(1,128)S(1)} %get-tuple-element.125), channel_id=1, source_target_pairs={{4,0},{5,1},{6,2},{7,3},{12,8},{13,9},{14,10},{15,11},{20,16},{21,... | collective-permute-start | bytes 776 | tf_op jit(solution)/shard_map/ppermute | solution.py:51
  73.1 7.3 copy-start.14
  73.6 6.9 copy-start.20
  73.7 120.1 %all-to-all-start.2 = ((bf16[4,320,1024]{2,1,0:T(8,128)(2,1)}), bf16[4,320,1024]{2,1,0:T(8,128)(2,1)}, u32[]{:S(2)}, u32[]{:S(2)}) async-start(bf16[4,320,1024]{2,1,0:T(8,128)(2,1)} %param.29), calls=%async_computation.2 | async-start | bytes 5242880 | tf_op jit(solution)/shard_map/all_to_all | solution.py:71
  78.5 418.5 %reduce-scatter.6.cloned.1.call-start = ((), (), s32[]{:S(2)}) async-start(), calls=%async_computation.8 | async-start | bytes 22216704 | tf_op jit(solution)/shard_map/reduce_scatter | solution.py:241
  79.2 2.3 copy-start
  79.6 16.6 %copy-start.16 = (f32[1024]{0:T(1024)}, f32[1024]{0:T(1024)S(1)}, u32[]{:S(2)}) copy-start(f32[1024]{0:T(1024)S(1)} %broadcast_multiply_fusion.8) | copy-start | bytes 12292
  80.4 15.8 %copy-start.18 = (f32[1024]{0:T(1024)}, f32[1024]{0:T(1024)S(1)}, u32[]{:S(2)}) copy-start(f32[1024]{0:T(1024)S(1)} %add_rsqrt_fusion.2) | copy-start | bytes 12292
  171.0 3.0 copy-start.6
  182.9 43.7 %copy-start.1 = (f32[1024,640]{1,0:T(8,128)}, f32[1024,640]{1,0:T(8,128)S(1)}, u32[]{:S(2)}) copy-start(f32[1024,640]{1,0:T(8,128)S(1)} %get-tuple-element.127) | copy-start | bytes 7864324
  190.8 1.1 copy-start.4
  191.8 30.4 %collective-permute-start.1 = (bf16[1,640,64]{1,2,0:T(8,128)(2,1)S(1)}, bf16[1,640,64]{1,2,0:T(8,128)(2,1)S(1)}, u32[]{:S(2)}, u32[]{:S(2)}) collective-permute-start(bf16[1,640,64]{1,2,0:T(8,128)(2,1)S(1)} %get-tuple-element.114), channel_id=1, source_target_pairs={{0,4},{1,5},{2,6},{3,7},{8,12},{9,13},{10,14},{11,15},{16,20},{17,... | collective-permute-start | bytes 245768 | tf_op jit(solution)/shard_map/ppermute | solution.py:50
  213.1 21.5 %collective-permute-start.3 = (bf16[1,640,64]{1,2,0:T(8,128)(2,1)S(1)}, bf16[1,640,64]{1,2,0:T(8,128)(2,1)S(1)}, u32[]{:S(2)}, u32[]{:S(2)}) collective-permute-start(bf16[1,640,64]{1,2,0:T(8,128)(2,1)S(1)} %get-tuple-element.113), channel_id=1, source_target_pairs={{4,0},{5,1},{6,2},{7,3},{12,8},{13,9},{14,10},{15,11},{20,16},{21,... | collective-permute-start | bytes 245768 | tf_op jit(solution)/shard_map/ppermute | solution.py:51
  222.2 2.9 copy-start.5
  256.2 12.4 %copy-start.8 = (f32[1024,640]{1,0:T(8,128)}, f32[1024,640]{1,0:T(8,128)S(1)}, u32[]{:S(2)}) copy-start(f32[1024,640]{1,0:T(8,128)S(1)} %get-tuple-element.129) | copy-start | bytes 7864324
  256.7 11.8 %copy-start.13 = (bf16[640,1280]{1,0:T(8,128)(2,1)S(1)}, bf16[640,1280]{1,0:T(8,128)(2,1)}, u32[]{:S(2)}) copy-start(bf16[640,1280]{1,0:T(8,128)(2,1)} %reshape.1474) | copy-start | bytes 4915204
  289.5 34.6 %collective-permute-start.5 = (bf16[1,640,64]{1,2,0:T(8,128)(2,1)S(1)}, bf16[1,640,64]{1,2,0:T(8,128)(2,1)S(1)}, u32[]{:S(2)}, u32[]{:S(2)}) collective-permute-start(bf16[1,640,64]{1,2,0:T(8,128)(2,1)S(1)} %get-tuple-element.111), channel_id=1, source_target_pairs={{0,4},{1,5},{2,6},{3,7},{8,12},{9,13},{10,14},{11,15},{16,20},{17,... | collective-permute-start | bytes 245768 | tf_op jit(solution)/shard_map/ppermute | solution.py:50
  292.6 30.6 %collective-permute-start.4 = (bf16[1,640,64]{1,2,0:T(8,128)(2,1)S(1)}, bf16[1,640,64]{1,2,0:T(8,128)(2,1)S(1)}, u32[]{:S(2)}, u32[]{:S(2)}) collective-permute-start(bf16[1,640,64]{1,2,0:T(8,128)(2,1)S(1)} %get-tuple-element.112), channel_id=1, source_target_pairs={{4,0},{5,1},{6,2},{7,3},{12,8},{13,9},{14,10},{15,11},{20,16},{21,... | collective-permute-start | bytes 245768 | tf_op jit(solution)/shard_map/ppermute | solution.py:51
  323.9 2.2 copy-start.12
  324.1 2.8 copy-start.2
  326.9 13.6 %copy-start.3 = (f32[1024,640]{1,0:T(8,128)S(1)}, f32[1024,640]{1,0:T(8,128)}, u32[]{:S(2)}) copy-start(f32[1024,640]{1,0:T(8,128)} %copy-done.1) | copy-start | bytes 7864324
  349.9 3.5 copy-start.15
  349.9 3.5 copy-start.17
  349.9 3.5 copy-start.19
  349.9 3.5 copy-start.21
  381.6 47.6 %copy-start.7 = (f32[4,204800]{1,0:T(4,128)S(1)}, f32[4,204800]{1,0:T(4,128)}, u32[]{:S(2)}) copy-start(f32[4,204800]{1,0:T(4,128)} %reshape.1493) | copy-start | bytes 9830404
  429.2 17.3 %copy-start.23 = (f32[4,320]{1,0:T(4,128)S(1)}, f32[4,320]{1,0:T(4,128)}, u32[]{:S(2)}) copy-start(f32[4,320]{1,0:T(4,128)} %convert_reduce_fusion.3) | copy-start | bytes 15364
  472.0 157.5 %reduce-scatter.8.cloned.1.call-start = ((), (), s32[]{:S(2)}) async-start(), calls=%async_computation.9 | async-start | bytes 9256960 | tf_op jit(solution)/shard_map/reduce_scatter | solution.py:242
  497.0 132.6 %copy-start.22 = (f32[4,320]{1,0:T(4,128)S(1)}, f32[4,320]{1,0:T(4,128)}, u32[]{:S(2)}) copy-start(f32[4,320]{1,0:T(4,128)} %get-tuple-element.122) | copy-start | bytes 15364
  497.0 170.1 %reduce-scatter.10.cloned.1.call-start = ((), (), s32[]{:S(2)}) async-start(), calls=%async_computation.11 | async-start | bytes 2314240
  629.5 121.9 %all-gather.7.cloned.1.call-start = ((), (), s32[]{:S(2)}) async-start(), calls=%async_computation.10 | async-start | bytes 4165632 | tf_op jit(solution)/shard_map/all_gather | solution.py:244
  629.7 37.5 %copy-start.9 = (f32[1024,640]{1,0:T(8,128)S(1)}, f32[1024,640]{1,0:T(8,128)}, u32[]{:S(2)}) copy-start(f32[1024,640]{1,0:T(8,128)} %copy-done.8) | copy-start | bytes 7864324
  682.4 35.4 %all-to-all-start.1 = ((bf16[4,1,320,1024]{3,2,1,0:T(8,128)(2,1)}), bf16[4,1,320,1024]{3,2,1,0:T(8,128)(2,1)}, u32[]{:S(2)}, u32[]{:S(2)}) async-start(bf16[4,1,320,1024]{3,2,1,0:T(8,128)(2,1)} %copy.62), calls=%async_computation.1 | async-start | bytes 5242880 | tf_op jit(solution)/shard_map/all_to_all | solution.py:76
  717.8 33.6 %all-to-all-start.3 = ((bf16[4,1,320,1024]{3,2,1,0:T(8,128)(2,1)}), bf16[4,1,320,1024]{3,2,1,0:T(8,128)(2,1)S(1)}, u32[]{:S(2)}, u32[]{:S(2)}) async-start(bf16[4,1,320,1024]{3,2,1,0:T(8,128)(2,1)} %copy.68), calls=%async_computation.3 | async-start | bytes 5242880 | tf_op jit(solution)/shard_map/all_to_all | solution.py:76
  751.4 3.2 copy-start.10
  765.6 3.6 copy-start.11
Sparse Core Ops, SparseCore 0:
  13.4 131.5 all-gather.4
  472.1 24.7 reduce-scatter.5
  499.4 130.0 reduce-scatter.7
  632.4 34.6 reduce-scatter.9
  668.5 42.8 all-gather.6
